TPU v7x, 32 devices: a whole 2x2x4 slice. The times are simulated.
32 devices in a mesh: group: 2 (over x), tp: 16 (over z, y, core), pool: 1.
Axes of the slice: x: 2, y: 2, z: 4, core: 2. Of those that a mesh axis runs over, the one named last changes fastest.
Arguments:
- prompt_x: bfloat16 [2048, 8192], P(('group', 'pool'), 'tp'), parts along dimension 0, may hold values from -6 to 6
- decode_x: bfloat16 [4, 32, 8192], P(None, ('group', 'pool'), 'tp'), parts along dimension 1, may hold values from -240 to 240
- w_query: bfloat16 [8192, 8192], P(None, 'tp'), may hold values from -0.0625 to 0.0625
- w_keyval: bfloat16 [8192, 2048], P('tp'), may hold values from -0.0625 to 0.0625
- w_out: bfloat16 [8192, 8192], P('tp'), may hold values from -0.0625 to 0.0625
- prompt_blocks: int32 [32], P('group'), parts along dimension 0, may hold values from 1 to 32, 64 in all
- prompt_row: int32 [32], P('group'), parts along dimension 0, may hold values from 0 to 15, each once
Outputs:
- decode_out: bfloat16 [4, 32, 8192], P(None, ('group', 'pool'), 'tp'), parts along dimension 1
There are 2 independent parts, one for each index of `group`. A program takes and returns all parts, laid end to end along the dimension named above; an argument that names none is the same for every part. Nothing has to cross between parts.
Inputs may be any that keep to these rules, and one draw needn't show every extreme that they name: `prompt_blocks`: each prompt has at least one block, the prompts fill the span exactly, and one prompt has exactly 32 blocks. `prompt_row`: every decode row continues exactly one prompt.
All inputs are finite; a program needn't handle non-finite values. Where the computation divides by a largest or mean magnitude, that divisor is 1e-20 or more.
Results may differ from a plain program's by a relative error of at most 0.018.
Values may be sent and summed in bfloat16 or wider, within the bound.
No kernel may reach another device: no remote copies, remote signals or barrier semaphores. Data moves between devices by JAX's collectives and lax.ppermute only.
A program may use at most 128 MiB of HBM per device.

v0:
```python
import math
import jax
import jax.numpy as jnp
import numpy as np
from jax import lax
from jax.sharding import PartitionSpec as P

KVH = 8
HD = 128
BLK = 16


def block_rows(prompt_blocks, prompt_row, total_blocks):
    block_ends = jnp.cumsum(prompt_blocks)
    positions = jnp.arange(total_blocks, dtype=jnp.int32)
    owner_seq = jnp.sum((block_ends[None, :] <= positions[:, None]).astype(jnp.int32), axis=1)
    seq_match = owner_seq[:, None] == jnp.arange(prompt_row.shape[0], dtype=jnp.int32)[None, :]
    return jnp.sum(jnp.where(seq_match, prompt_row[None, :], 0), axis=1)


def attend(queries, cache_vals, cache_scale, slot_row, fresh_keyval, row_ids):
    head_dim = queries.shape[-1]
    inverse_root = 1.0 / math.sqrt(head_dim)
    query_f32 = queries.astype(jnp.float32)
    scale_f32 = cache_scale.astype(jnp.float32)
    cache_keys = cache_vals[:, :, :head_dim].astype(jnp.float32) * scale_f32[:, 0][:, None, None]
    cache_values = cache_vals[:, :, head_dim:].astype(jnp.float32) * scale_f32[:, 1][:, None, None]
    cache_score = jnp.einsum("srgd,nkd->srgnk", query_f32, cache_keys) * inverse_root
    visible = slot_row[None, :] == row_ids[:, None]
    cache_score = jnp.where(visible[None, :, None, :, None], cache_score, -jnp.inf)
    fresh_f32 = fresh_keyval.astype(jnp.float32)
    fresh_score = jnp.einsum("srgd,trd->srgt", query_f32, fresh_f32[:, :, :head_dim]) * inverse_root
    step_index = jnp.arange(queries.shape[0], dtype=jnp.int32)
    causal = step_index[:, None] >= step_index[None, :]
    fresh_score = jnp.where(causal[:, None, None, :], fresh_score, -jnp.inf)
    top_score = jnp.maximum(jnp.max(cache_score, axis=(3, 4)), jnp.max(fresh_score, axis=3))
    cache_weight = jnp.exp(cache_score - top_score[..., None, None])
    fresh_weight = jnp.exp(fresh_score - top_score[..., None])
    denominator = jnp.sum(cache_weight, axis=(3, 4)) + jnp.sum(fresh_weight, axis=3)
    weighted = jnp.einsum("srgnk,nkd->srgd", cache_weight, cache_values)
    weighted = weighted + jnp.einsum("srgt,trd->srgd", fresh_weight, fresh_f32[:, :, head_dim:])
    return weighted / denominator[..., None]


def on_device(prompt_x, decode_x, w_query, w_keyval, w_out, prompt_blocks, prompt_row):
    tp_count = lax.axis_size("tp")
    pool_count = lax.axis_size("pool")
    tp_index = lax.axis_index("tp")
    pool_index = lax.axis_index("pool")
    half_tokens = prompt_x.shape[0]
    tokens_here = half_tokens // tp_count
    blocks_here = tokens_here // BLK
    half_blocks = half_tokens // BLK
    total_blocks = half_blocks * pool_count
    keyval = lax.psum_scatter(
        jnp.dot(prompt_x, w_keyval, preferred_element_type=jnp.float32),
        "tp",
        scatter_dimension=0,
        tiled=True,
    )
    blocked = keyval.reshape(blocks_here, BLK, KVH, 2, HD)
    scales = (jnp.max(jnp.abs(blocked), axis=(1, 4)) + 1e-06).astype(jnp.bfloat16)
    stored = (blocked / scales.astype(jnp.float32)[:, None, :, :, None]).astype(jnp.bfloat16)
    stored = stored.reshape(blocks_here, BLK, KVH, 2 * HD)
    slot_row_all = block_rows(prompt_blocks, prompt_row, total_blocks)
    row_half = decode_x.shape[1]
    owner_half = slot_row_all // row_half
    first_block = pool_index * half_blocks + tp_index * blocks_here
    mine_owner = lax.dynamic_slice_in_dim(owner_half, first_block, blocks_here, 0)
    dest_head = np.arange(tp_count) * KVH // tp_count
    by_head = stored.transpose(2, 0, 1, 3)[dest_head]
    scale_head = scales.transpose(1, 0, 2)[dest_head]
    to_half = mine_owner[None, :] == jnp.arange(pool_count, dtype=jnp.int32)[:, None]
    zero_value = jnp.zeros((), jnp.bfloat16)
    send_vals = jnp.where(to_half[None, :, :, None, None], by_head[:, None], zero_value)
    send_scale = jnp.where(to_half[None, :, :, None], scale_head[:, None], zero_value)
    got_vals, got_scale = (
        lax.all_to_all(
            lax.all_to_all(send_vals, "tp", split_axis=0, concat_axis=0, tiled=True),
            "pool",
            split_axis=1,
            concat_axis=1,
            tiled=True,
        ),
        lax.all_to_all(
            lax.all_to_all(send_scale, "tp", split_axis=0, concat_axis=0, tiled=True),
            "pool",
            split_axis=1,
            concat_axis=1,
            tiled=True,
        ),
    )
    got_vals = got_vals.reshape(total_blocks, BLK, 2 * HD)
    got_scale = got_scale.reshape(total_blocks, 2)
    slot_row = (
        slot_row_all.reshape(pool_count, tp_count, blocks_here)
        .transpose(1, 0, 2)
        .reshape(total_blocks)
    )
    gathered = lax.all_gather(decode_x, "tp", axis=2, tiled=True)
    step_count, row_count, model_width = gathered.shape
    heads_here = w_query.shape[1] // HD
    queries = jnp.einsum("srd,de->sre", gathered, w_query, preferred_element_type=jnp.float32)
    queries = queries.astype(jnp.bfloat16).reshape(step_count, row_count, heads_here, HD)
    partial_new = jnp.einsum("srd,de->sre", decode_x, w_keyval, preferred_element_type=jnp.float32)
    summed_new = lax.psum(partial_new, "tp")
    fresh_keyval = summed_new.astype(jnp.bfloat16).reshape(step_count, row_count, KVH, 2 * HD)
    my_head = tp_index * KVH // tp_count
    fresh_keyval = lax.dynamic_index_in_dim(fresh_keyval, my_head, 2, keepdims=False)
    row_ids = pool_index * row_count + jnp.arange(row_count, dtype=jnp.int32)
    weighted = attend(queries, got_vals, got_scale, slot_row, fresh_keyval, row_ids)
    attended = weighted.reshape(step_count, row_count, heads_here * HD).astype(jnp.bfloat16)
    out_term = jnp.einsum("sre,ed->srd", attended, w_out, preferred_element_type=jnp.float32)
    return lax.psum_scatter(out_term, "tp", scatter_dimension=2, tiled=True).astype(jnp.bfloat16)


def solution(mesh):
    placed = (
        P(("group", "pool"), "tp"),
        P(None, ("group", "pool"), "tp"),
        P(None, "tp"),
        P("tp", None),
        P("tp", None),
        P("group"),
        P("group"),
    )
    return jax.shard_map(
        on_device,
        mesh=mesh,
        in_specs=placed,
        out_specs=P(None, ("group", "pool"), "tp"),
        check_vma=False,
    )
```

profile of v0, /device:TPU:0, one launch (start us, length us, event | category | flops | bytes accessed | tf_op | source)
XLA Modules:
  0.0 254.8 jit_solution(7903377930404320485)
XLA Ops:
  6.5 1.6 copy-done
  8.1 6.8 %fusion.50 = f32[1024,2048]{1,0:T(8,128)} fusion(bf16[1024,512]{1,0:T(8,128)(2,1)} %param.10, bf16[512,2048]{1,0:T(8,128)(2,1)S(1)} %copy-done), kind=kOutput, calls=%fused_computation.76 | convolution fusion | flops 2147483648 | bytes 11534336 | tf_op jit(solution)/shard_map/dot_general | solution.py:56
  15.0 0.7 all-gather.2.cloned.1.call-update
  15.8 0.5 fusion.4
  16.3 74.8 %all-reduce.1 = bf16[4,16,2048]{2,1,0:T(8,128)(2,1)S(1)} all-reduce(f32[4,16,2048]{2,1,0:T(8,128)S(1)} %fusion.4), channel_id=1, replica_groups=mesh['group'=2,'tp'=16,'pool'=1] {'tp'}, use_global_device_ids=true, to_apply=%region_6.7 | all-reduce | flops 131072 | bytes 786432 | tf_op jit(solution)/shard_map/psum | solution.py:106
  91.8 32.1 %reduce-scatter.3.cloned.1.call-done = f32[64,2048]{1,0:T(8,128)} async-done(((f32[1024,2048]{1,0:T(8,128)}), f32[64,2048]{1,0:T(8,128)}) %reduce-scatter.3.cloned.1.call-update) | async-done | bytes 524304 | tf_op jit(solution)/shard_map/reduce_scatter | solution.py:55
  123.8 1.9 abs.6
  125.8 1.5 abs.7
  128.3 0.6 gather_fusion
  128.9 0.6 gather_fusion.1
  129.7 0.7 copy.98
  130.4 4.3 %all-to-all-start.1 = ((bf16[16,1,4,2]{2,3,1,0:T(2,128)(2,1)}), bf16[16,1,4,2]{2,3,1,0:T(2,128)(2,1)S(1)}, u32[]{:S(2)}, u32[]{:S(2)}) async-start(bf16[16,1,4,2]{2,3,1,0:T(2,128)(2,1)} %copy.98), calls=%async_computation.2 | async-start | bytes 16384 | tf_op jit(solution)/shard_map/all_to_all | solution.py:86
  134.7 0.9 fusion.26
  135.6 5.5 %all-to-all-done.1 = bf16[16,1,4,2]{2,3,1,0:T(2,128)(2,1)S(1)} async-done(((bf16[16,1,4,2]{2,3,1,0:T(2,128)(2,1)}), bf16[16,1,4,2]{2,3,1,0:T(2,128)(2,1)S(1)}, u32[]{:S(2)}, u32[]{:S(2)}) %all-to-all-start.1) | async-done | bytes 288 | tf_op jit(solution)/shard_map/all_to_all | solution.py:86
  141.1 3.6 %all-to-all-start = ((bf16[16,1,4,16,256]{4,3,2,1,0:T(8,128)(2,1)}), bf16[16,1,4,16,256]{4,3,2,1,0:T(8,128)(2,1)S(1)}, u32[]{:S(2)}, u32[]{:S(2)}) async-start(bf16[16,1,4,16,256]{4,3,2,1,0:T(8,128)(2,1)} %fusion.26), calls=%async_computation.1 | async-start | bytes 1048576 | tf_op jit(solution)/shard_map/all_to_all | solution.py:79
  144.8 20.9 %all-gather.2.cloned.1.call-done = bf16[4,16,8192]{2,1,0:T(8,128)(2,1)} async-done(((bf16[4,16,512]{2,1,0:T(8,128)(2,1)}), bf16[4,16,8192]{2,1,0:T(8,128)(2,1)}) %all-gather.2.cloned.1.call-update) | async-done | bytes 1048592 | tf_op jit(solution)/shard_map/all_gather | solution.py:100
  165.7 5.3 %fusion.15 = bf16[4,16,512]{2,1,0:T(8,128)(2,1)S(1)} fusion(bf16[4,16,8192]{2,1,0:T(8,128)(2,1)} %all-gather.2.cloned.1.call-done, bf16[8192,512]{1,0:T(8,128)(2,1)} %param.12), kind=kOutput, calls=%fused_computation.20 | convolution fusion | flops 536903680 | bytes 9502720 | tf_op jit(solution)/shard_map/srd,de->sre/dot_general | solution.py:103
  171.0 0.7 fusion.49
  172.2 1.9 fusion.6
  174.6 2.2 fusion.7
  176.9 2.3 fusion.18
  179.2 6.3 %fusion = f32[4,16,8192]{2,1,0:T(8,128)} fusion(bf16[512,8192]{1,0:T(8,128)(2,1)} %param.14, bf16[4,4,2,8,128]{4,3,2,1,0:T(8,128)(2,1)S(1)} %fusion.18), kind=kOutput, calls=%fused_computation.2 | convolution fusion | flops 536870912 | bytes 10551296 | tf_op jit(solution)/shard_map/sre,ed->srd/dot_general | solution.py:113
  185.6 61.2 %reduce-scatter.5.cloned.1.call-done = f32[4,16,512]{2,1,0:T(8,128)} async-done(((f32[4,16,8192]{2,1,0:T(8,128)}), f32[4,16,512]{2,1,0:T(8,128)}) %reduce-scatter.5.cloned.1.call-update) | async-done | bytes 131088 | tf_op jit(solution)/shard_map/reduce_scatter | solution.py:114
  246.8 1.5 convert_element_type.67
  (54 shorter events, 3.2 us)
Async XLA Ops:
  6.5 1.6 copy-start
  6.5 117.3 %reduce-scatter.3.cloned.1.call-start = ((), (), s32[]{:S(2)}) async-start(), calls=%async_computation.5 | async-start | bytes 8912896 | tf_op jit(solution)/shard_map/reduce_scatter | solution.py:55
  14.9 0.8 copy-start.2
  14.9 150.7 %all-gather.2.cloned.1.call-start = ((), (), s32[]{:S(2)}) async-start(), calls=%async_computation.4 | async-start | bytes 1114112 | tf_op jit(solution)/shard_map/all_gather | solution.py:100
  15.7 75.5 %copy-start.3 = (s32[16]{0:T(128)S(1)}, s32[16]{0:T(128)}, u32[]{:S(2)}) copy-start(s32[16]{0:T(128)} %param.15) | copy-start | bytes 196
  15.8 75.8 %copy-start.5 = (s32[16]{0:T(128)S(1)}, s32[16]{0:T(128)}, u32[]{:S(2)}) copy-start(s32[16]{0:T(128)} %param.16) | copy-start | bytes 196
  15.8 76.0 %copy-start.4 = (s32[16]{0:T(128)S(1)}, s32[16]{0:T(128)}, u32[]{:S(2)}) copy-start(s32[16]{0:T(128)} %constant.66) | copy-start | bytes 196
  123.8 4.0 %copy-start.1 = (f32[64,2048]{1,0:T(8,128)S(1)}, f32[64,2048]{1,0:T(8,128)}, u32[]{:S(2)}) copy-start(f32[64,2048]{1,0:T(8,128)} %reduce-scatter.3.cloned.1.call-done) | copy-start | bytes 1572868
  130.4 10.8 %all-to-all-start.1 = ((bf16[16,1,4,2]{2,3,1,0:T(2,128)(2,1)}), bf16[16,1,4,2]{2,3,1,0:T(2,128)(2,1)S(1)}, u32[]{:S(2)}, u32[]{:S(2)}) async-start(bf16[16,1,4,2]{2,3,1,0:T(2,128)(2,1)} %copy.98), calls=%async_computation.2 | async-start | bytes 16384 | tf_op jit(solution)/shard_map/all_to_all | solution.py:86
  141.1 31.0 %all-to-all-start = ((bf16[16,1,4,16,256]{4,3,2,1,0:T(8,128)(2,1)}), bf16[16,1,4,16,256]{4,3,2,1,0:T(8,128)(2,1)S(1)}, u32[]{:S(2)}, u32[]{:S(2)}) async-start(bf16[16,1,4,16,256]{4,3,2,1,0:T(8,128)(2,1)} %fusion.26), calls=%async_computation.1 | async-start | bytes 1048576 | tf_op jit(solution)/shard_map/all_to_all | solution.py:79
  144.7 102.1 %reduce-scatter.5.cloned.1.call-start = ((), (), s32[]{:S(2)}) async-start(), calls=%async_computation.6 | async-start | bytes 2228224 | tf_op jit(solution)/shard_map/reduce_scatter | solution.py:114
Sparse Core Ops, SparseCore 0:
  15.1 108.7 reduce-scatter.2
  126.0 39.6 all-gather.1
  185.7 61.0 reduce-scatter.4
where the time goes:
time: 255 us
  waiting for transfers between devices  120 us (47%)
  blocking collectives  74.8 us (29%)
  matrix products  24 us (9%)
  between operations  13.3 us (5%)
  starting transfers between devices  7.99 us (3%)
  other arithmetic  7.65 us (3%)
  local copies, waits for them, and re-layouts  6.69 us (3%)
    psum x1, blocking collectives, on_device(): summed_new = lax.psum(partial_new, 'tp')  74.8 us
    reduce_scatter x1, waiting for transfers between devices, on_device(): lax.psum_scatter(out_term, 'tp', scatter_dimension=2, tiled=True)  61.2 us
    reduce_scatter x1, waiting for transfers between devices, on_device(): lax.psum_scatter(jnp.dot(prompt_x, w_keyval, preferred_element_type=jnp.f...  32.1 us
    all_gather x1, waiting for transfers between devices, on_device(): gathered = lax.all_gather(decode_x, 'tp', axis=2, tiled=True)  20.9 us
    dot_general x1, matrix products, on_device(): jnp.dot(prompt_x, w_keyval, preferred_element_type=jnp.float32)  6.79 us
    dot_general x1, matrix products, on_device(): jnp.einsum('sre,ed->srd', attended, w_out, preferred_element_type=jnp.flo...  6.33 us
    all_to_all x1, waiting for transfers between devices, on_device(): lax.all_to_all(send_scale, 'tp', split_axis=0, concat_axis=0, tiled=True)  5.52 us
    dot_general x1, matrix products, on_device(): jnp.einsum('srd,de->sre', gathered, w_query, preferred_element_type=jnp.f...  5.27 us
  transfers between devices with their start and end apart: 5, of which 4 were waited for; matrix products, arithmetic and copies ran while one was open for 6% of the time, Pallas kernels for 0%

commit v1 on v0

--- a/solution.py
+++ b/solution.py
@@ -103,7 +103,7 @@
     queries = jnp.einsum("srd,de->sre", gathered, w_query, preferred_element_type=jnp.float32)
     queries = queries.astype(jnp.bfloat16).reshape(step_count, row_count, heads_here, HD)
     partial_new = jnp.einsum("srd,de->sre", decode_x, w_keyval, preferred_element_type=jnp.float32)
-    summed_new = lax.psum(partial_new, "tp")
+    summed_new = jnp.sum(lax.all_gather(partial_new, "tp"), axis=0)
     fresh_keyval = summed_new.astype(jnp.bfloat16).reshape(step_count, row_count, KVH, 2 * HD)
     my_head = tp_index * KVH // tp_count
     fresh_keyval = lax.dynamic_index_in_dim(fresh_keyval, my_head, 2, keepdims=False)

time: 255 us -> 323 us (1.27)
  waiting for transfers between devices: 120 us -> 259 us
  blocking collectives: 74.8 us -> 0 us
  other arithmetic: 7.65 us -> 11.9 us
    psum x1 -> x0, blocking collectives: 74.8 us -> none  [on_device(): summed_new = lax.psum(partial_new, 'tp')]
    reduce_scatter x1, waiting for transfers between devices: 32.1 us -> 104 us  [on_device(): lax.psum_scatter(jnp.dot(prompt_x, w_keyval, preferred_element_type=jnp.f...]
    all_gather x0 -> x1, waiting for transfers between devices: none -> 68 us  [on_device(): summed_new = jnp.sum(lax.all_gather(partial_new, 'tp'), axis=0)]
    reduce_sum x0 -> x1, other arithmetic: none -> 3.96 us  [on_device(): summed_new = jnp.sum(lax.all_gather(partial_new, 'tp'), axis=0)]
  transfers between devices with their start and end apart: 5 -> 6, of which waited for: 4 -> 5; matrix products, arithmetic and copies ran while one was open for 6% -> 5% of each run, Pallas kernels for 0% -> 0%
where the time goes in v1:
time: 323 us; the launch traced here: 322 us
  waiting for transfers between devices  259 us (80%)
  matrix products  23.3 us (7%)
  between operations  13.3 us (4%)
  other arithmetic  11.9 us (4%)
  starting transfers between devices  8.05 us (2%)
  local copies, waits for them, and re-layouts  6.66 us (2%)
    reduce_scatter x1, waiting for transfers between devices, on_device(): lax.psum_scatter(jnp.dot(prompt_x, w_keyval, preferred_element_type=jnp.f...  104 us
    all_gather x1, waiting for transfers between devices, on_device(): summed_new = jnp.sum(lax.all_gather(partial_new, 'tp'), axis=0)  68 us
    reduce_scatter x1, waiting for transfers between devices, on_device(): lax.psum_scatter(out_term, 'tp', scatter_dimension=2, tiled=True)  60.5 us
    all_gather x1, waiting for transfers between devices, on_device(): gathered = lax.all_gather(decode_x, 'tp', axis=2, tiled=True)  20.9 us
    dot_general x1, matrix products, on_device(): jnp.dot(prompt_x, w_keyval, preferred_element_type=jnp.float32)  6.77 us
  transfers between devices with their start and end apart: 6, of which 5 were waited for; matrix products, arithmetic and copies ran while one was open for 5% of the time, Pallas kernels for 0%

profile of v1, /device:TPU:0, one launch (start us, length us, event | category | flops | bytes accessed | tf_op | source)
XLA Modules:
  0.0 322.4 jit_solution(2951061519129435480)
XLA Ops:
  6.5 1.6 copy-done
  8.1 6.8 %fusion.50 = f32[1024,2048]{1,0:T(8,128)} fusion(bf16[1024,512]{1,0:T(8,128)(2,1)} %param.10, bf16[512,2048]{1,0:T(8,128)(2,1)S(1)} %copy-done), kind=kOutput, calls=%fused_computation.76 | convolution fusion | flops 2147483648 | bytes 11534336 | tf_op jit(solution)/shard_map/dot_general | solution.py:56
  15.0 0.7 all-gather.4.cloned.1.call-update
  15.8 1.3 fusion.4
  17.7 103.6 %reduce-scatter.3.cloned.1.call-done = f32[64,2048]{1,0:T(8,128)} async-done(((f32[1024,2048]{1,0:T(8,128)}), f32[64,2048]{1,0:T(8,128)}) %reduce-scatter.3.cloned.1.call-update) | async-done | bytes 524304 | tf_op jit(solution)/shard_map/reduce_scatter | solution.py:55
  121.3 2.0 abs.6
  123.3 1.5 abs.7
  126.4 0.6 gather_fusion.1
  127.1 0.7 copy.97
  127.8 4.4 %all-to-all-start.1 = ((bf16[16,1,4,2]{2,3,1,0:T(2,128)(2,1)}), bf16[16,1,4,2]{2,3,1,0:T(2,128)(2,1)S(1)}, u32[]{:S(2)}, u32[]{:S(2)}) async-start(bf16[16,1,4,2]{2,3,1,0:T(2,128)(2,1)} %copy.97), calls=%async_computation.2 | async-start | bytes 16384 | tf_op jit(solution)/shard_map/all_to_all | solution.py:86
  132.2 1.0 fusion.26
  133.2 5.4 %all-to-all-done.1 = bf16[16,1,4,2]{2,3,1,0:T(2,128)(2,1)S(1)} async-done(((bf16[16,1,4,2]{2,3,1,0:T(2,128)(2,1)}), bf16[16,1,4,2]{2,3,1,0:T(2,128)(2,1)S(1)}, u32[]{:S(2)}, u32[]{:S(2)}) %all-to-all-start.1) | async-done | bytes 288 | tf_op jit(solution)/shard_map/all_to_all | solution.py:86
  138.6 3.6 %all-to-all-start = ((bf16[16,1,4,16,256]{4,3,2,1,0:T(8,128)(2,1)}), bf16[16,1,4,16,256]{4,3,2,1,0:T(8,128)(2,1)S(1)}, u32[]{:S(2)}, u32[]{:S(2)}) async-start(bf16[16,1,4,16,256]{4,3,2,1,0:T(8,128)(2,1)} %fusion.26), calls=%async_computation.1 | async-start | bytes 1048576 | tf_op jit(solution)/shard_map/all_to_all | solution.py:79
  142.2 20.9 %all-gather.4.cloned.1.call-done = bf16[4,16,8192]{2,1,0:T(8,128)(2,1)} async-done(((bf16[4,16,512]{2,1,0:T(8,128)(2,1)}), bf16[4,16,8192]{2,1,0:T(8,128)(2,1)}) %all-gather.4.cloned.1.call-update) | async-done | bytes 1048592 | tf_op jit(solution)/shard_map/all_gather | solution.py:100
  163.1 5.3 %fusion.15 = bf16[4,16,512]{2,1,0:T(8,128)(2,1)S(1)} fusion(bf16[4,16,8192]{2,1,0:T(8,128)(2,1)} %all-gather.4.cloned.1.call-done, bf16[8192,512]{1,0:T(8,128)(2,1)} %param.12), kind=kOutput, calls=%fused_computation.20 | convolution fusion | flops 536903680 | bytes 9502720 | tf_op jit(solution)/shard_map/srd,de->sre/dot_general | solution.py:103
  168.8 1.9 fusion.6
  170.8 68.0 %all-gather.6.cloned.1.call-done = f32[64,16,2048]{2,1,0:T(8,128)} async-done(((f32[4,16,2048]{2,1,0:T(8,128)}), f32[64,16,2048]{2,1,0:T(8,128)}) %all-gather.6.cloned.1.call-update) | async-done | bytes 8388624 | tf_op jit(solution)/shard_map/all_gather | solution.py:106
  238.8 4.0 %reduce_sum.47 = bf16[4,16,2048]{2,1,0:T(8,128)(2,1)S(1)} reduce(f32[16,4,16,2048]{3,2,1,0:T(8,128)} %bitcast.97, f32[]{:T(128)} %constant.62.clone.1), dimensions={0}, to_apply=%region_6.7 | reduce | flops 1966080 | bytes 8650756 | tf_op jit(solution)/shard_map/reduce_sum | solution.py:106
  242.9 0.7 fusion.49
  244.3 2.4 fusion.7
  246.7 0.7 fusion.18
  247.4 6.3 %fusion = f32[4,16,8192]{2,1,0:T(8,128)} fusion(bf16[512,8192]{1,0:T(8,128)(2,1)} %param.14, bf16[4,4,2,8,128]{4,3,2,1,0:T(8,128)(2,1)S(1)} %fusion.18), kind=kOutput, calls=%fused_computation.2 | convolution fusion | flops 536870912 | bytes 10551296 | tf_op jit(solution)/shard_map/sre,ed->srd/dot_general | solution.py:113
  253.8 60.5 %reduce-scatter.5.cloned.1.call-done = f32[4,16,512]{2,1,0:T(8,128)} async-done(((f32[4,16,8192]{2,1,0:T(8,128)}), f32[4,16,512]{2,1,0:T(8,128)}) %reduce-scatter.5.cloned.1.call-update) | async-done | bytes 131088 | tf_op jit(solution)/shard_map/reduce_scatter | solution.py:114
  314.3 1.5 convert_element_type.72
  (59 shorter events, 3.8 us)
Async XLA Ops:
  6.5 1.6 copy-start
  6.5 114.7 %reduce-scatter.3.cloned.1.call-start = ((), (), s32[]{:S(2)}) async-start(), calls=%async_computation.5 | async-start | bytes 8912896 | tf_op jit(solution)/shard_map/reduce_scatter | solution.py:55
  14.9 0.9 copy-start.3
  14.9 2.2 copy-start.4
  14.9 2.5 copy-start.6
  15.0 2.7 copy-start.5
  15.0 148.2 %all-gather.4.cloned.1.call-start = ((), (), s32[]{:S(2)}) async-start(), calls=%async_computation.4 | async-start | bytes 1114112 | tf_op jit(solution)/shard_map/all_gather | solution.py:100
  15.7 223.0 %all-gather.6.cloned.1.call-start = ((), (), s32[]{:S(2)}) async-start(), calls=%async_computation.7 | async-start | bytes 8912896 | tf_op jit(solution)/shard_map/all_gather | solution.py:106
  121.3 4.1 %copy-start.2 = (f32[64,2048]{1,0:T(8,128)S(1)}, f32[64,2048]{1,0:T(8,128)}, u32[]{:S(2)}) copy-start(f32[64,2048]{1,0:T(8,128)} %reduce-scatter.3.cloned.1.call-done) | copy-start | bytes 1572868
  127.8 10.7 %all-to-all-start.1 = ((bf16[16,1,4,2]{2,3,1,0:T(2,128)(2,1)}), bf16[16,1,4,2]{2,3,1,0:T(2,128)(2,1)S(1)}, u32[]{:S(2)}, u32[]{:S(2)}) async-start(bf16[16,1,4,2]{2,3,1,0:T(2,128)(2,1)} %copy.97), calls=%async_computation.2 | async-start | bytes 16384 | tf_op jit(solution)/shard_map/all_to_all | solution.py:86
  138.6 30.2 %all-to-all-start = ((bf16[16,1,4,16,256]{4,3,2,1,0:T(8,128)(2,1)}), bf16[16,1,4,16,256]{4,3,2,1,0:T(8,128)(2,1)S(1)}, u32[]{:S(2)}, u32[]{:S(2)}) async-start(bf16[16,1,4,16,256]{4,3,2,1,0:T(8,128)(2,1)} %fusion.26), calls=%async_computation.1 | async-start | bytes 1048576 | tf_op jit(solution)/shard_map/all_to_all | solution.py:79
  142.1 172.1 %reduce-scatter.5.cloned.1.call-start = ((), (), s32[]{:S(2)}) async-start(), calls=%async_computation.6 | async-start | bytes 2228224 | tf_op jit(solution)/shard_map/reduce_scatter | solution.py:114
  244.3 2.4 copy-start.1
Sparse Core Ops, SparseCore 0:
  15.0 106.1 reduce-scatter.2
  123.4 39.6 all-gather.3
  165.3 73.4 all-gather.5
  253.9 60.3 reduce-scatter.4
